TPU v7x, 32 devices: a whole 2x2x4 slice. The times are simulated.
32 devices in a mesh: snap: 8 (over z, x), feat: 4 (over y, core).
Axes of the slice: x: 2, y: 2, z: 4, core: 2. Of those that a mesh axis runs over, the one named last changes fastest.
Arguments:
- node_features: bfloat16 [16, 512, 256], P('snap', None, 'feat'), may hold values from -6 to 6
- tile_rows: int32 [16, 8], P('snap'), may hold values from 0 to 3
- tile_cols: int32 [16, 8], P('snap'), may hold values from 0 to 3, as said below
- tile_counts: int32 [16], P('snap'), may hold values from 4 to 8, as said below
- tile_values: bfloat16 [16, 8, 128, 128], P('snap'), may hold values from -0.5 to 0.5
- layer_one: bfloat16 [256, 256], replicated, may hold values from -0.375 to 0.375
- layer_two: bfloat16 [256, 256], replicated, may hold values from -0.375 to 0.375
- query_weight: bfloat16 [256, 256], replicated, may hold values from -1.25 to 1.25
- key_weight: bfloat16 [256, 256], replicated, may hold values from -1.25 to 1.25
- value_weight: bfloat16 [256, 256], replicated, may hold values from -0.375 to 0.375
- out_weight: bfloat16 [256, 256], replicated, may hold values from -0.375 to 0.375
Outputs:
- evolved: bfloat16 [16, 512, 256], P('snap', None, 'feat')
Inputs may be any that keep to these rules, and one draw needn't show every extreme that they name: `tile_cols`: block columns of the tile slots; a coordinate pair may be listed more than once, and such tiles add. `tile_counts`: some snapshot uses all 8 slots.
All inputs are finite; a program needn't handle non-finite values.
Results may differ from a plain program's by a relative error of at most 0.02.
The roundings to bfloat16 on the way count: a program that leaves them out, or rounds other values in their place, can miss the bound.
Values may be sent and summed in bfloat16 or wider, within the bound.
A program may use at most 64 MiB of HBM per device.

v0:
```python
import jax
import jax.numpy as jnp
from jax import lax
from jax.sharding import PartitionSpec as P

HEADS = 8
masked_score = -1e30


def spread_padded(features, tile_block, block_rows, block_cols, slot_count):
    vert_count, feat_width = features.shape
    tile_side = tile_block.shape[1]
    slot_total = tile_block.shape[0]
    block_count = vert_count // tile_side
    blocked = features.reshape(block_count, tile_side, feat_width)
    picked_blocks = blocked[block_cols]
    live_slots = jnp.arange(slot_total, dtype=jnp.int32) < slot_count
    products = jnp.einsum(
        "irc,icf->irf", tile_block, picked_blocks, preferred_element_type=jnp.float32
    )
    products = products * live_slots.astype(jnp.float32)[:, None, None]
    membership = (
        (block_rows[None, :] == jnp.arange(block_count, dtype=jnp.int32)[:, None])
        & live_slots[None, :]
    ).astype(jnp.float32)
    summed = jnp.dot(
        membership,
        products.reshape(slot_total, tile_side * feat_width),
        precision=lax.Precision.HIGHEST,
    )
    return summed.reshape(vert_count, feat_width).astype(jnp.bfloat16)


def attend_local(hidden, query_weight, key_weight, value_weight, out_weight):
    snaps, verts, model_width = hidden.shape
    head_dim = model_width // HEADS
    flat = hidden.reshape(snaps * verts, model_width)

    def project(weight):
        return (
            jnp.dot(flat, weight, preferred_element_type=jnp.float32)
            .astype(jnp.bfloat16)
            .reshape(snaps, verts, HEADS, head_dim)
        )

    query_heads = project(query_weight)
    key_heads = project(key_weight)
    value_heads = project(value_weight)
    scores = jnp.einsum(
        "tvhd,uvhd->vhtu", query_heads, key_heads, preferred_element_type=jnp.float32
    ) * head_dim ** (-0.5)
    causal = (
        jnp.arange(snaps, dtype=jnp.int32)[:, None] >= jnp.arange(snaps, dtype=jnp.int32)[None, :]
    )
    scores = jnp.where(causal, scores, masked_score)
    row_max = jnp.max(scores, axis=-1, keepdims=True)
    lifted = jnp.exp(scores - row_max)
    weights = (lifted / jnp.sum(lifted, axis=-1, keepdims=True)).astype(jnp.bfloat16)
    context = jnp.einsum(
        "vhtu,uvhd->tvhd", weights, value_heads, preferred_element_type=jnp.float32
    ).astype(jnp.bfloat16)
    context = context.reshape(snaps * verts, model_width)
    result = flat.astype(jnp.float32) + jnp.dot(
        context, out_weight, preferred_element_type=jnp.float32
    )
    return result.astype(jnp.bfloat16).reshape(snaps, verts, model_width)


def on_device(
    node_features,
    tile_rows,
    tile_cols,
    tile_counts,
    tile_values,
    layer_one,
    layer_two,
    query_weight,
    key_weight,
    value_weight,
    out_weight,
):
    snap_dev, vert_count, feat_width = node_features.shape
    feat_index = lax.axis_index("feat")

    def spread_all(features):
        spread_pieces = []
        for snapshot in range(snap_dev):
            spread_pieces.append(
                spread_padded(
                    features[snapshot],
                    tile_values[snapshot],
                    tile_rows[snapshot],
                    tile_cols[snapshot],
                    tile_counts[snapshot],
                )
            )
        return jnp.stack(spread_pieces, axis=0)

    def convolve(features, weight):
        spread_rows = spread_all(features).reshape(snap_dev * vert_count, feat_width)
        own_columns = lax.dynamic_slice_in_dim(weight, feat_index * feat_width, feat_width, 1)
        mixed_sum = jnp.dot(
            lax.all_gather(spread_rows, "feat", axis=1, tiled=True),
            own_columns,
            preferred_element_type=jnp.float32,
        )
        mixed_sum = mixed_sum.reshape(snap_dev, vert_count, feat_width)
        return (features.astype(jnp.float32) + jnp.maximum(mixed_sum, 0.0)).astype(jnp.bfloat16)

    hidden_one = convolve(node_features, layer_one)
    hidden_two = convolve(hidden_one, layer_two)
    vertex_rows = lax.all_to_all(
        lax.all_to_all(hidden_two, "snap", split_axis=1, concat_axis=0, tiled=True),
        "feat",
        split_axis=1,
        concat_axis=2,
        tiled=True,
    )
    attended = attend_local(vertex_rows, query_weight, key_weight, value_weight, out_weight)
    return lax.all_to_all(
        lax.all_to_all(attended, "feat", split_axis=2, concat_axis=1, tiled=True),
        "snap",
        split_axis=0,
        concat_axis=1,
        tiled=True,
    )


def solution(mesh):
    placed = (
        P("snap", None, "feat"),
        P("snap", None),
        P("snap", None),
        P("snap"),
        P("snap", None, None, None),
        P(),
        P(),
        P(),
        P(),
        P(),
        P(),
    )
    return jax.shard_map(
        on_device, mesh=mesh, in_specs=placed, out_specs=P("snap", None, "feat"), check_vma=False
    )
```

profile of v0, /device:TPU:0, one launch (start us, length us, event | category | flops | bytes accessed | tf_op | source)
XLA Modules:
  0.0 81.3 jit_solution(12368943352257759503)
XLA Ops:
  0.0 0.7 copy-done.9
  0.7 0.9 %fusion.47 = (bf16[1,512,64]{1,2,0:T(8,128)(2,1)S(1)}, bf16[1,512,64]{1,2,0:T(8,128)(2,1)S(1)}) fusion(bf16[2,512,64]{1,2,0:T(8,128)(2,1)} %param.11), kind=kLoop, calls=%fused_computation.79 | loop fusion | bytes 262144 | tf_op jit(solution)/shard_map/slice | solution.py:90
  1.7 0.6 copy-done.8
  2.4 0.6 fusion.48
  3.0 0.6 iota_compare_fusion.4
  3.6 0.6 gather_fusion
  4.2 0.3 fusion.8
  4.9 0.5 copy-done.10
  5.4 0.2 convolution_convert_fusion.3
  5.9 0.6 iota_compare_fusion.3
  6.5 0.6 gather_fusion.1
  7.1 0.3 fusion.7
  7.8 0.2 convolution_convert_fusion.2
  8.4 8.7 %all_gather.6 = bf16[1024,256]{0,1:T(8,128)(2,1)S(1)} all-gather(bf16[1024,64]{0,1:T(8,128)(2,1)S(1)} %copy.107), channel_id=1, replica_groups=mesh['snap'=8,'feat'=4] {'feat'}, dimensions={1}, use_global_device_ids=true | all-gather | bytes 655360 | tf_op jit(solution)/shard_map/all_gather | solution.py:103
  17.1 0.3 convolution_maximum_fusion.1
  17.4 0.6 copy-done.2
  18.1 0.6 gather_fusion.2
  18.6 0.3 fusion.6
  19.3 0.2 convolution_convert_fusion.1
  19.8 0.6 gather_fusion.3
  20.4 0.3 fusion.5
  21.0 0.2 convolution_convert_fusion
  21.7 7.4 %all_gather.7 = bf16[1024,256]{0,1:T(8,128)(2,1)S(1)} all-gather(bf16[1024,64]{0,1:T(8,128)(2,1)S(1)} %copy.113), channel_id=1, replica_groups=mesh['snap'=8,'feat'=4] {'feat'}, dimensions={1}, use_global_device_ids=true | all-gather | bytes 655360 | tf_op jit(solution)/shard_map/all_gather | solution.py:103
  29.1 0.3 convolution_maximum_fusion
  29.6 0.2 reshape.211
  29.9 13.1 %all_to_all.69 = bf16[8,2,4096]{2,1,0:T(2,128)(2,1)S(1)} all-to-all(bf16[8,2,4096]{2,1,0:T(2,128)(2,1)S(1)} %reshape.211), channel_id=1, replica_groups=mesh['snap'=8,'feat'=4] {'snap'}, dimensions={0} | all-to-all | bytes 262144 | tf_op jit(solution)/shard_map/all_to_all | solution.py:113
  43.4 0.9 %reshape.213 = bf16[4,2,8192]{2,1,0:T(2,128)(2,1)} reshape(bf16[64,16,64]{2,1,0:T(8,128)(2,1)S(1)} %bitcast.111) | data formatting | bytes 262144
  44.3 3.3 %all-to-all-start.1 = ((bf16[4,2,8192]{2,1,0:T(2,128)(2,1)}), bf16[4,2,8192]{2,1,0:T(2,128)(2,1)S(1)}, u32[]{:S(2)}, u32[]{:S(2)}) async-start(bf16[4,2,8192]{2,1,0:T(2,128)(2,1)} %reshape.213), calls=%async_computation.1 | async-start | bytes 262144 | tf_op jit(solution)/shard_map/all_to_all | solution.py:112
  47.7 4.6 %all-to-all-done.1 = bf16[4,2,8192]{2,1,0:T(2,128)(2,1)S(1)} async-done(((bf16[4,2,8192]{2,1,0:T(2,128)(2,1)}), bf16[4,2,8192]{2,1,0:T(2,128)(2,1)S(1)}, u32[]{:S(2)}, u32[]{:S(2)}) %all-to-all-start.1) | async-done | bytes 131104 | tf_op jit(solution)/shard_map/all_to_all | solution.py:112
  52.7 0.2 reshape.173
  52.9 0.7 copy-done.3
  53.8 0.2 reshape.175
  54.0 0.7 copy-done.4
  54.9 0.2 reshape.176
  55.1 0.7 copy-done.5
  55.9 0.2 reshape.174
  56.2 1.0 %fusion.49 = (f32[16,8,16]{2,1,0:T(8,128)S(1)}, f32[16,8,16,16]{2,3,1,0:T(8,128)S(1)}) fusion(bf16[16,16,8,32]{3,2,1,0:T(8,128)(2,1)S(1)} %reshape.176, bf16[16,16,8,32]{3,2,1,0:T(8,128)(2,1)S(1)} %reshape.175, pred[16,16]{0,1:T(8,128)(4,1)S(1)} %iota_compare_fusion), kind=kOutput, calls=%fused_computation.81 | convolution fusion | flops 2228239 | bytes 401664 | tf_op jit(solution)/shard_map/sub | solution.py:57
  57.2 0.5 fusion.4
  57.9 0.4 reshape.177
  58.3 0.5 copy-done.6
  59.0 0.9 %copy.126 = bf16[16,16,256]{1,0,2:T(8,128)(2,1)S(1)} copy(bf16[16,16,256]{2,1,0:T(8,128)(2,1)S(1)} %bitcast.115) | data formatting | bytes 262144 | tf_op jit(solution)/shard_map/reshape | solution.py:66
  60.0 1.1 %reshape.215 = bf16[4,2,8192]{2,1,0:T(2,128)(2,1)S(1)} reshape(bf16[256,16,16]{2,1,0:T(8,128)(2,1)S(1)} %bitcast.102) | data formatting | bytes 262144
  61.0 7.0 %all_to_all.70 = bf16[4,2,8192]{2,1,0:T(2,128)(2,1)S(1)} all-to-all(bf16[4,2,8192]{2,1,0:T(2,128)(2,1)S(1)} %reshape.215), channel_id=1, replica_groups=mesh['snap'=8,'feat'=4] {'feat'}, dimensions={0} | all-to-all | bytes 262144 | tf_op jit(solution)/shard_map/all_to_all | solution.py:121
  68.0 0.7 reshape.216
  68.7 1.2 %copy.134 = bf16[16,16,4,64]{3,2,1,0:T(4,128)(2,1)S(1)} copy(bf16[16,16,4,64]{1,0,3,2:T(8,128)(2,1)S(1)} %bitcast.101) | data formatting | bytes 262144 | tf_op jit(solution)/shard_map/all_to_all | solution.py:121
  69.9 0.2 reshape.217
  70.2 9.9 %all_to_all.71 = bf16[8,2,4096]{2,1,0:T(2,128)(2,1)S(1)} all-to-all(bf16[8,2,4096]{2,1,0:T(2,128)(2,1)S(1)} %reshape.217), channel_id=1, replica_groups=mesh['snap'=8,'feat'=4] {'snap'}, dimensions={0} | all-to-all | bytes 262144 | tf_op jit(solution)/shard_map/all_to_all | solution.py:120
  80.5 0.9 %all_to_all.64 = bf16[2,512,64]{1,2,0:T(8,128)(2,1)} reshape(bf16[2,8,64,64]{2,1,3,0:T(8,128)(2,1)S(1)} %copy.129) | data formatting | bytes 262144 | tf_op jit(solution)/shard_map/all_to_all | solution.py:120
  (59 shorter events, 5.2 us)
Async XLA Ops:
  0.0 17.1 %copy-start = (bf16[256,256]{1,0:T(8,128)(2,1)S(1)}, bf16[256,256]{1,0:T(8,128)(2,1)}, u32[]{:S(2)}) copy-start(bf16[256,256]{1,0:T(8,128)(2,1)} %param.16) | copy-start | bytes 393220
  0.0 0.7 copy-start.9
  0.7 3.5 %copy-start.1 = (bf16[2,8,128,128]{3,2,1,0:T(8,128)(2,1)S(1)}, bf16[2,8,128,128]{3,2,1,0:T(8,128)(2,1)}, u32[]{:S(2)}) copy-start(bf16[2,8,128,128]{3,2,1,0:T(8,128)(2,1)} %param.15) | copy-start | bytes 1572868
  1.7 0.7 copy-start.8
  4.7 0.7 copy-start.10
  17.1 0.9 %copy-start.2 = (bf16[2,512,64]{1,2,0:T(8,128)(2,1)S(1)}, bf16[2,512,64]{1,2,0:T(8,128)(2,1)}, u32[]{:S(2)}) copy-start(bf16[2,512,64]{1,2,0:T(8,128)(2,1)} %param.11) | copy-start | bytes 393220
  21.7 7.4 %copy-start.7 = (bf16[256,256]{1,0:T(8,128)(2,1)S(1)}, bf16[256,256]{1,0:T(8,128)(2,1)}, u32[]{:S(2)}) copy-start(bf16[256,256]{1,0:T(8,128)(2,1)} %param.17) | copy-start | bytes 393220
  44.3 7.9 %all-to-all-start.1 = ((bf16[4,2,8192]{2,1,0:T(2,128)(2,1)}), bf16[4,2,8192]{2,1,0:T(2,128)(2,1)S(1)}, u32[]{:S(2)}, u32[]{:S(2)}) async-start(bf16[4,2,8192]{2,1,0:T(2,128)(2,1)} %reshape.213), calls=%async_computation.1 | async-start | bytes 262144 | tf_op jit(solution)/shard_map/all_to_all | solution.py:112
  52.7 0.9 %copy-start.3 = (bf16[256,256]{1,0:T(8,128)(2,1)S(1)}, bf16[256,256]{1,0:T(8,128)(2,1)}, u32[]{:S(2)}) copy-start(bf16[256,256]{1,0:T(8,128)(2,1)} %param.18) | copy-start | bytes 393220
  53.8 0.9 %copy-start.4 = (bf16[256,256]{1,0:T(8,128)(2,1)S(1)}, bf16[256,256]{1,0:T(8,128)(2,1)}, u32[]{:S(2)}) copy-start(bf16[256,256]{1,0:T(8,128)(2,1)} %param.19) | copy-start | bytes 393220
  54.9 0.9 %copy-start.5 = (bf16[256,256]{1,0:T(8,128)(2,1)S(1)}, bf16[256,256]{1,0:T(8,128)(2,1)}, u32[]{:S(2)}) copy-start(bf16[256,256]{1,0:T(8,128)(2,1)} %param.20) | copy-start | bytes 393220
  57.9 0.9 %copy-start.6 = (bf16[256,256]{1,0:T(8,128)(2,1)S(1)}, bf16[256,256]{1,0:T(8,128)(2,1)}, u32[]{:S(2)}) copy-start(bf16[256,256]{1,0:T(8,128)(2,1)} %param.21) | copy-start | bytes 393220
where the time goes:
time: 81.8 us; the launch traced here: 81.3 us
  blocking collectives  46 us (56%)
  local copies, waits for them, and re-layouts  20.4 us (25%)
  matrix products  4.96 us (6%)
  waiting for transfers between devices  4.55 us (6%)
  starting transfers between devices  3.33 us (4%)
  other arithmetic  1.48 us (2%)
    all_gather x2, blocking collectives, convolve(): lax.all_gather(spread_rows, 'feat', axis=1, tiled=True)  16.1 us
    all_to_all x1, blocking collectives, on_device(): lax.all_to_all(hidden_two, 'snap', split_axis=1, concat_axis=0, tiled=True)  13.1 us
    all_to_all x1, blocking collectives, on_device(): lax.all_to_all(lax.all_to_all(attended, 'feat', split_axis=2, concat_axis...  9.86 us
    unnamed x30, local copies, waits for them, and re-layouts  8.75 us
    all_to_all x1, blocking collectives, on_device(): lax.all_to_all(attended, 'feat', split_axis=2, concat_axis=1, tiled=True)  6.99 us
    all_to_all x1, waiting for transfers between devices, on_device(): lax.all_to_all(lax.all_to_all(hidden_two, 'snap', split_axis=1, concat_ax...  4.55 us
    all_to_all x1, starting transfers between devices, on_device(): lax.all_to_all(lax.all_to_all(hidden_two, 'snap', split_axis=1, concat_ax...  3.33 us
    gather x4, local copies, waits for them, and re-layouts, spread_padded(): picked_blocks = blocked[block_cols]  2.29 us
  transfers between devices with their start and end apart: 1, of which 1 were waited for; matrix products, arithmetic and copies ran while one was open for 0% of the time, Pallas kernels for 0%

commit v1 on v0

--- a/solution.py
+++ b/solution.py
@@ -5,6 +5,13 @@
 
 HEADS = 8
 masked_score = -1e30
+
+
+def swap_blocks(block, axis, split, join):
+    count = lax.axis_size(axis)
+    blocks = jnp.stack(jnp.split(block, count, axis=split), axis=0)
+    blocks = lax.all_to_all(blocks, axis, split_axis=0, concat_axis=0)
+    return jnp.concatenate(blocks, axis=join)
 
 
 def spread_padded(features, tile_block, block_rows, block_cols, slot_count):
@@ -117,12 +124,8 @@
         tiled=True,
     )
     attended = attend_local(vertex_rows, query_weight, key_weight, value_weight, out_weight)
-    return lax.all_to_all(
-        lax.all_to_all(attended, "feat", split_axis=2, concat_axis=1, tiled=True),
-        "snap",
-        split_axis=0,
-        concat_axis=1,
-        tiled=True,
+    return swap_blocks(
+        lax.all_to_all(attended, "feat", split_axis=2, concat_axis=1, tiled=True), "snap", 0, 1
     )
 
 

time: 81.8 us -> 82 us (level)
    all_to_all x2 -> x0, local copies, waits for them, and re-layouts: 1.07 us -> none  [on_device(): lax.all_to_all(lax.all_to_all(attended, 'feat', split_axis=2, concat_axis...]
    reshape x0 -> x2, local copies, waits for them, and re-layouts: none -> 1.07 us  [swap_blocks(): return jnp.concatenate(blocks, axis=join)]
    unnamed x30 -> x37, local copies, waits for them, and re-layouts: 8.75 us -> 8.81 us
where the time goes in v1:
time: 82 us; the launch traced here: 81.5 us
  blocking collectives  46 us (56%)
  local copies, waits for them, and re-layouts  20.6 us (25%)
  matrix products  4.97 us (6%)
  waiting for transfers between devices  4.55 us (6%)
  starting transfers between devices  3.33 us (4%)
  other arithmetic  1.39 us (2%)
    all_gather x2, blocking collectives, convolve(): lax.all_gather(spread_rows, 'feat', axis=1, tiled=True)  16.1 us
    all_to_all x1, blocking collectives, on_device(): lax.all_to_all(hidden_two, 'snap', split_axis=1, concat_axis=0, tiled=True)  13.1 us
    all_to_all x1, blocking collectives, swap_blocks(): blocks = lax.all_to_all(blocks, axis, split_axis=0, concat_axis=0)  9.85 us
    unnamed x37, local copies, waits for them, and re-layouts  8.81 us
    all_to_all x1, blocking collectives, on_device(): lax.all_to_all(attended, 'feat', split_axis=2, concat_axis=1, tiled=True)  6.99 us
    all_to_all x1, waiting for transfers between devices, on_device(): lax.all_to_all(lax.all_to_all(hidden_two, 'snap', split_axis=1, concat_ax...  4.55 us
    all_to_all x1, starting transfers between devices, on_device(): lax.all_to_all(lax.all_to_all(hidden_two, 'snap', split_axis=1, concat_ax...  3.33 us
    gather x4, local copies, waits for them, and re-layouts, spread_padded(): picked_blocks = blocked[block_cols]  2.29 us
  transfers between devices with their start and end apart: 1, of which 1 were waited for; matrix products, arithmetic and copies ran while one was open for 0% of the time, Pallas kernels for 0%

profile of v1, /device:TPU:0, one launch (start us, length us, event | category | flops | bytes accessed | tf_op | source)
XLA Modules:
  0.0 81.5 jit_solution(8275645558342450618)
XLA Ops:
  0.0 0.7 copy-done.9
  0.7 0.9 %fusion.48 = (bf16[1,512,64]{1,2,0:T(8,128)(2,1)S(1)}, bf16[1,512,64]{1,2,0:T(8,128)(2,1)S(1)}) fusion(bf16[2,512,64]{1,2,0:T(8,128)(2,1)} %param.11), kind=kLoop, calls=%fused_computation.88 | loop fusion | bytes 262144 | tf_op jit(solution)/shard_map/slice | solution.py:97
  1.7 0.6 copy-done.8
  2.4 0.6 fusion.49
  2.9 0.6 iota_compare_fusion.4
  3.6 0.6 gather_fusion
  4.2 0.3 fusion.8
  4.9 0.5 copy-done.10
  5.3 0.2 convolution_convert_fusion.3
  5.8 0.5 iota_compare_fusion.3
  6.4 0.6 gather_fusion.1
  6.9 0.3 fusion.7
  7.6 0.2 convolution_convert_fusion.2
  8.2 8.7 %all_gather.6 = bf16[1024,256]{0,1:T(8,128)(2,1)S(1)} all-gather(bf16[1024,64]{0,1:T(8,128)(2,1)S(1)} %copy.136), channel_id=1, replica_groups=mesh['snap'=8,'feat'=4] {'feat'}, dimensions={1}, use_global_device_ids=true | all-gather | bytes 655360 | tf_op jit(solution)/shard_map/all_gather | solution.py:110
  16.9 0.3 convolution_maximum_fusion.1
  17.2 0.6 copy-done.2
  17.9 0.6 gather_fusion.2
  18.5 0.3 fusion.6
  19.2 0.2 convolution_convert_fusion.1
  19.6 0.6 gather_fusion.3
  20.2 0.3 fusion.5
  20.9 0.2 convolution_convert_fusion
  21.5 7.4 %all_gather.7 = bf16[1024,256]{0,1:T(8,128)(2,1)S(1)} all-gather(bf16[1024,64]{0,1:T(8,128)(2,1)S(1)} %copy.142), channel_id=1, replica_groups=mesh['snap'=8,'feat'=4] {'feat'}, dimensions={1}, use_global_device_ids=true | all-gather | bytes 655360 | tf_op jit(solution)/shard_map/all_gather | solution.py:110
  29.0 0.3 convolution_maximum_fusion
  29.5 0.2 reshape.235
  29.7 13.1 %all_to_all.53 = bf16[8,2,4096]{2,1,0:T(2,128)(2,1)S(1)} all-to-all(bf16[8,2,4096]{2,1,0:T(2,128)(2,1)S(1)} %reshape.235), channel_id=1, replica_groups=mesh['snap'=8,'feat'=4] {'snap'}, dimensions={0} | all-to-all | bytes 262144 | tf_op jit(solution)/shard_map/all_to_all | solution.py:120
  43.3 0.9 %reshape.237 = bf16[4,2,8192]{2,1,0:T(2,128)(2,1)} reshape(bf16[64,16,64]{2,1,0:T(8,128)(2,1)S(1)} %bitcast.116) | data formatting | bytes 262144
  44.2 3.3 %all-to-all-start.1 = ((bf16[4,2,8192]{2,1,0:T(2,128)(2,1)}), bf16[4,2,8192]{2,1,0:T(2,128)(2,1)S(1)}, u32[]{:S(2)}, u32[]{:S(2)}) async-start(bf16[4,2,8192]{2,1,0:T(2,128)(2,1)} %reshape.237), calls=%async_computation.1 | async-start | bytes 262144 | tf_op jit(solution)/shard_map/all_to_all | solution.py:119
  47.5 4.6 %all-to-all-done.1 = bf16[4,2,8192]{2,1,0:T(2,128)(2,1)S(1)} async-done(((bf16[4,2,8192]{2,1,0:T(2,128)(2,1)}), bf16[4,2,8192]{2,1,0:T(2,128)(2,1)S(1)}, u32[]{:S(2)}, u32[]{:S(2)}) %all-to-all-start.1) | async-done | bytes 131104 | tf_op jit(solution)/shard_map/all_to_all | solution.py:119
  52.5 0.2 reshape.195
  52.7 0.7 copy-done.3
  53.6 0.2 reshape.197
  53.9 0.7 copy-done.4
  54.7 0.2 reshape.198
  55.0 0.7 copy-done.5
  55.8 0.2 reshape.196
  56.1 1.0 %fusion.50 = (f32[16,8,16]{2,1,0:T(8,128)S(1)}, f32[16,8,16,16]{2,3,1,0:T(8,128)S(1)}) fusion(bf16[16,16,8,32]{3,2,1,0:T(8,128)(2,1)S(1)} %reshape.198, bf16[16,16,8,32]{3,2,1,0:T(8,128)(2,1)S(1)} %reshape.197, pred[16,16]{0,1:T(8,128)(4,1)S(1)} %iota_compare_fusion), kind=kOutput, calls=%fused_computation.90 | convolution fusion | flops 2228239 | bytes 401664 | tf_op jit(solution)/shard_map/sub | solution.py:64
  57.1 0.5 fusion.4
  57.8 0.4 reshape.199
  58.1 0.5 copy-done.6
  58.9 0.9 %copy.155 = bf16[16,16,256]{1,0,2:T(8,128)(2,1)S(1)} copy(bf16[16,16,256]{2,1,0:T(8,128)(2,1)S(1)} %bitcast.119) | data formatting | bytes 262144 | tf_op jit(solution)/shard_map/reshape | solution.py:73
  59.8 1.1 %reshape.239 = bf16[4,2,8192]{2,1,0:T(2,128)(2,1)S(1)} reshape(bf16[256,16,16]{2,1,0:T(8,128)(2,1)S(1)} %bitcast.107) | data formatting | bytes 262144
  60.9 7.0 %all_to_all.54 = bf16[4,2,8192]{2,1,0:T(2,128)(2,1)S(1)} all-to-all(bf16[4,2,8192]{2,1,0:T(2,128)(2,1)S(1)} %reshape.239), channel_id=1, replica_groups=mesh['snap'=8,'feat'=4] {'feat'}, dimensions={0} | all-to-all | bytes 262144 | tf_op jit(solution)/shard_map/all_to_all | solution.py:128
  67.9 0.7 reshape.240
  68.6 1.2 %copy.170 = bf16[16,16,4,64]{3,2,1,0:T(4,128)(2,1)S(1)} copy(bf16[16,16,4,64]{1,0,3,2:T(8,128)(2,1)S(1)} %bitcast.106) | data formatting | bytes 262144 | tf_op jit(solution)/shard_map/all_to_all | solution.py:128
  70.1 0.2 reshape.241
  70.3 9.9 %all_to_all.55 = bf16[8,2,4096]{2,1,0:T(2,128)(2,1)S(1)} all-to-all(bf16[8,2,4096]{2,1,0:T(2,128)(2,1)S(1)} %reshape.241), channel_id=1, replica_groups=mesh['snap'=8,'feat'=4] {'snap'}, dimensions={0} | all-to-all | bytes 262144 | tf_op jit(solution)/shard_map/all_to_all | solution.py:13
  80.6 0.9 %reshape.202 = bf16[2,512,64]{1,2,0:T(8,128)(2,1)} reshape(bf16[2,8,64,64]{2,1,3,0:T(8,128)(2,1)S(1)} %copy.165) | data formatting | bytes 262144 | tf_op jit(solution)/shard_map/reshape | solution.py:14
  (75 shorter events, 5.4 us)
Async XLA Ops:
  0.0 16.9 %copy-start = (bf16[256,256]{1,0:T(8,128)(2,1)S(1)}, bf16[256,256]{1,0:T(8,128)(2,1)}, u32[]{:S(2)}) copy-start(bf16[256,256]{1,0:T(8,128)(2,1)} %param.16) | copy-start | bytes 393220
  0.0 0.7 copy-start.9
  0.7 3.4 %copy-start.1 = (bf16[2,8,128,128]{3,2,1,0:T(8,128)(2,1)S(1)}, bf16[2,8,128,128]{3,2,1,0:T(8,128)(2,1)}, u32[]{:S(2)}) copy-start(bf16[2,8,128,128]{3,2,1,0:T(8,128)(2,1)} %param.15) | copy-start | bytes 1572868
  1.7 0.7 copy-start.8
  4.7 0.7 copy-start.10
  16.9 0.9 %copy-start.2 = (bf16[2,512,64]{1,2,0:T(8,128)(2,1)S(1)}, bf16[2,512,64]{1,2,0:T(8,128)(2,1)}, u32[]{:S(2)}) copy-start(bf16[2,512,64]{1,2,0:T(8,128)(2,1)} %param.11) | copy-start | bytes 393220
  21.5 7.4 %copy-start.7 = (bf16[256,256]{1,0:T(8,128)(2,1)S(1)}, bf16[256,256]{1,0:T(8,128)(2,1)}, u32[]{:S(2)}) copy-start(bf16[256,256]{1,0:T(8,128)(2,1)} %param.17) | copy-start | bytes 393220
  44.2 7.9 %all-to-all-start.1 = ((bf16[4,2,8192]{2,1,0:T(2,128)(2,1)}), bf16[4,2,8192]{2,1,0:T(2,128)(2,1)S(1)}, u32[]{:S(2)}, u32[]{:S(2)}) async-start(bf16[4,2,8192]{2,1,0:T(2,128)(2,1)} %reshape.237), calls=%async_computation.1 | async-start | bytes 262144 | tf_op jit(solution)/shard_map/all_to_all | solution.py:119
  52.5 0.9 %copy-start.3 = (bf16[256,256]{1,0:T(8,128)(2,1)S(1)}, bf16[256,256]{1,0:T(8,128)(2,1)}, u32[]{:S(2)}) copy-start(bf16[256,256]{1,0:T(8,128)(2,1)} %param.18) | copy-start | bytes 393220
  53.6 0.9 %copy-start.4 = (bf16[256,256]{1,0:T(8,128)(2,1)S(1)}, bf16[256,256]{1,0:T(8,128)(2,1)}, u32[]{:S(2)}) copy-start(bf16[256,256]{1,0:T(8,128)(2,1)} %param.19) | copy-start | bytes 393220
  54.7 0.9 %copy-start.5 = (bf16[256,256]{1,0:T(8,128)(2,1)S(1)}, bf16[256,256]{1,0:T(8,128)(2,1)}, u32[]{:S(2)}) copy-start(bf16[256,256]{1,0:T(8,128)(2,1)} %param.20) | copy-start | bytes 393220
  57.8 0.9 %copy-start.6 = (bf16[256,256]{1,0:T(8,128)(2,1)S(1)}, bf16[256,256]{1,0:T(8,128)(2,1)}, u32[]{:S(2)}) copy-start(bf16[256,256]{1,0:T(8,128)(2,1)} %param.21) | copy-start | bytes 393220
